TPU v7x, 512 devices: a whole 4x8x8 slice. The times are simulated.
512 devices in a mesh: gx: 32 (over y_hi, z, core), yz: 16 (over x, y_lo).
Axes of the slice: x: 4, y: 8 (y_hi: 2, y_lo: 4; y = y_hi * 4 + y_lo), z: 8, core: 2. Of those that a mesh axis runs over, the one named last changes fastest.
Arguments:
- gauge_links: float32 [64, 2, 3, 3, 2048], P('gx', None, None, None, 'yz'), may hold values from -1 to 1, as said below
- in_field: float32 [8, 64, 2, 3, 3, 2048], P(None, 'gx', None, None, None, 'yz'), may hold values from -6 to 6
- cotangent: float32 [8, 64, 2, 3, 3, 2048], P(None, 'gx', None, None, None, 'yz'), may hold values from -6 to 6
- bilinear_weights: float32 [8, 8, 24, 8], replicated, may hold values from -0.15625 to 0.15625
Outputs:
- grad_field: float32 [8, 64, 2, 3, 3, 2048], P(None, 'gx', None, None, None, 'yz')
- grad_weights: float32 [8, 8, 24, 8], replicated
Inputs may be any that keep to these rules, and one draw needn't show every extreme that they name: `gauge_links`: every site's link is a special unitary 3 x 3 matrix (unitary with determinant 1), stored as real and imaginary parts.
All inputs are finite; a program needn't handle non-finite values.
Results may differ from a plain program's by a relative error of at most 0.0003.
Values sent between devices are 32-bit elements; how exact they have to be, the bound alone decides.
No kernel may reach another device: no remote copies, remote signals or barrier semaphores. Data moves between devices by JAX's collectives and lax.ppermute only.
A program may use at most 64 MiB of HBM per device.

v0:
```python
import math
import jax
import jax.numpy as jnp
from jax import lax
from jax.sharding import PartitionSpec as P


def from_behind(block, axis, distance):
    devices = range(lax.axis_size(axis))
    route = [((i - distance) % len(devices), i) for i in devices]
    return lax.ppermute(block, axis, route)


def matmul_three(left, right):
    return jnp.sum(left[..., :, :, None, :] * right[..., None, :, :, :], axis=-3)


def complex_mul(left, right):
    left_re = left[..., 0, :, :, :]
    left_im = left[..., 1, :, :, :]
    right_re = right[..., 0, :, :, :]
    right_im = right[..., 1, :, :, :]
    real_part = matmul_three(left_re, right_re) - matmul_three(left_im, right_im)
    imag_part = matmul_three(left_re, right_im) + matmul_three(left_im, right_re)
    return jnp.stack([real_part, imag_part], axis=-4)


def dagger(matrix):
    swapped = jnp.swapaxes(matrix, -3, -2)
    return jnp.stack([swapped[..., 0, :, :, :], -swapped[..., 1, :, :, :]], axis=-4)


def per_device(gauge_links, in_field, cotangent, bilinear_weights):
    part_x = gauge_links.shape[0]
    channels = in_field.shape[0]
    line_count = bilinear_weights.shape[2]
    site_count = gauge_links.shape[-1]
    reach_devs = (part_x - 1 + line_count) // part_x
    highest = lax.Precision.HIGHEST
    weight_rows = bilinear_weights.reshape(channels * channels, line_count * channels)

    def advance(carry, unused):
        arrived = from_behind(carry, "gx", -1)
        return (arrived, arrived)

    unused_last, stacked = lax.scan(advance, (gauge_links, in_field), None, length=reach_devs)
    window_links = jnp.concatenate(
        [gauge_links, stacked[0].reshape((-1, 2, 3, 3, site_count))], axis=0
    )
    later_field = jnp.moveaxis(stacked[1], 0, 1).reshape((channels, -1, 2, 3, 3, site_count))
    window_field = jnp.concatenate([in_field, later_field], axis=1)
    pair_grad = complex_mul(dagger(in_field)[None], cotangent[:, None]).reshape(
        channels * channels, -1
    )

    def forward_step(line, offset):
        shifted = lax.dynamic_slice_in_dim(window_field, offset, part_x, axis=1)
        transported = complex_mul(complex_mul(line[None], shifted), dagger(line)[None])
        next_links = lax.dynamic_slice_in_dim(window_links, offset, part_x, axis=0)
        return (complex_mul(line, next_links), (transported, line))

    offsets = jnp.arange(1, line_count + 1, dtype=jnp.int32)
    unused_line, (all_transported, all_lines) = lax.scan(forward_step, gauge_links, offsets)
    transported_flat = all_transported.reshape(line_count * channels, -1)
    partial_grad = lax.dot_general(
        pair_grad, transported_flat, (((1,), (1,)), ((), ())), precision=highest
    )
    mixed = jnp.dot(weight_rows, transported_flat, precision=highest)
    mixed_matrix = mixed.reshape((channels, channels) + in_field.shape[1:])
    direct = jnp.sum(complex_mul(cotangent[:, None], dagger(mixed_matrix)), axis=0)
    line_grad = jnp.dot(weight_rows.T, pair_grad, precision=highest)
    line_grad = line_grad.reshape((line_count,) + in_field.shape)
    accumulator = jnp.zeros((channels, (reach_devs + 1) * part_x, 2, 3, 3, site_count), jnp.float32)

    def backward_step(carry, inputs):
        offset, grad_piece, line = inputs
        contribution = complex_mul(complex_mul(dagger(line)[None], grad_piece), line[None])
        current = lax.dynamic_slice_in_dim(carry, offset, part_x, axis=1)
        return (
            lax.dynamic_update_slice_in_dim(carry, current + contribution, offset, axis=1),
            None,
        )

    accumulator, unused_out = lax.scan(backward_step, accumulator, (offsets, line_grad, all_lines))
    blocks = jnp.moveaxis(
        accumulator.reshape((channels, reach_devs + 1, part_x, 2, 3, 3, site_count)), 1, 0
    )

    def return_step(carry, block):
        arrived = from_behind(carry, "gx", 1)
        return (arrived + block, None)

    far_terms, unused_tail = lax.scan(return_step, blocks[reach_devs], blocks[:reach_devs][::-1])
    grad_field = direct + far_terms
    total_x = part_x * lax.axis_size("gx")
    total_sites = site_count * lax.axis_size("yz")
    summed = lax.psum(partial_grad, ("gx", "yz"))
    grad_weights = summed.reshape(channels, channels, line_count, channels) / math.sqrt(
        100.0 * total_x * total_sites
    )
    return (grad_field, grad_weights)


def solution(mesh):
    placed = (
        P("gx", None, None, None, "yz"),
        P(None, "gx", None, None, None, "yz"),
        P(None, "gx", None, None, None, "yz"),
        P(),
    )
    return jax.shard_map(
        per_device,
        mesh=mesh,
        in_specs=placed,
        out_specs=(P(None, "gx", None, None, None, "yz"), P()),
        check_vma=False,
    )
```

profile of v0, /device:TPU:2, one launch (start us, length us, event | category | flops | bytes accessed | tf_op | source)
XLA Modules:
  0.0 771.0 jit_solution(7964423564091880756)
XLA Ops:
  2.4 183.7 %while.50 = (s32[]{:T(128)}, f32[2,2,3,3,128]{4,1,3,2,0:T(2,128)S(1)}, f32[8,2,2,3,3,128]{5,2,4,3,1,0:T(2,128)S(1)}, f32[12,2,2,3,3,128]{5,1,0,4,3,2:T(2,128)S(1...) while((s32[]{:T(128)}, f32[2,2,3,3,128]{4,1,3,2,0:T(2,128)S(1)}, ...), condition=%wide.region_1.2_spmd, body=%wide.region_0.1_spmd.sunk | while | flops 2 | bytes 1327269 | solution.py:46
  2.4 15.6 %collective-permute-start = (f32[2,2,3,3,128]{4,1,3,2,0:T(2,128)S(1)}, f32[2,2,3,3,128]{4,1,3,2,0:T(2,128)S(1)}, u32[]{:S(2)}, u32[]{:S(2)}) collective-permute-start(f32[2,2,3,3,128]{4,1,3,2,0:T(2,128)S(1)} %get-tuple-element.507), channel_id=1, source_target_pairs={{16,0},{32,16},{48,32},{64,48},{80,64},{96,80},{112,96},{128,112},... | collective-permute-start | bytes 55304 | tf_op jit(solution)/shard_map/while/body/eval_jaxpr/ppermute | solution.py:11
  18.0 2.6 collective-permute-start.1
  20.6 4.2 collective-permute-done.1
  24.9 9.8 %collective-permute-start = (f32[2,2,3,3,128]{4,1,3,2,0:T(2,128)S(1)}, f32[2,2,3,3,128]{4,1,3,2,0:T(2,128)S(1)}, u32[]{:S(2)}, u32[]{:S(2)}) collective-permute-start(f32[2,2,3,3,128]{4,1,3,2,0:T(2,128)S(1)} %get-tuple-element.507), channel_id=1, source_target_pairs={{16,0},{32,16},{48,32},{64,48},{80,64},{96,80},{112,96},{128,112},... | collective-permute-start | bytes 55304 | tf_op jit(solution)/shard_map/while/body/eval_jaxpr/ppermute | solution.py:11
  34.7 1.9 collective-permute-start.1
  36.7 3.9 collective-permute-done.1
  40.8 9.8 %collective-permute-start = (f32[2,2,3,3,128]{4,1,3,2,0:T(2,128)S(1)}, f32[2,2,3,3,128]{4,1,3,2,0:T(2,128)S(1)}, u32[]{:S(2)}, u32[]{:S(2)}) collective-permute-start(f32[2,2,3,3,128]{4,1,3,2,0:T(2,128)S(1)} %get-tuple-element.507), channel_id=1, source_target_pairs={{16,0},{32,16},{48,32},{64,48},{80,64},{96,80},{112,96},{128,112},... | collective-permute-start | bytes 55304 | tf_op jit(solution)/shard_map/while/body/eval_jaxpr/ppermute | solution.py:11
  50.6 1.9 collective-permute-start.1
  52.6 2.7 collective-permute-done.1
  55.4 9.8 %collective-permute-start = (f32[2,2,3,3,128]{4,1,3,2,0:T(2,128)S(1)}, f32[2,2,3,3,128]{4,1,3,2,0:T(2,128)S(1)}, u32[]{:S(2)}, u32[]{:S(2)}) collective-permute-start(f32[2,2,3,3,128]{4,1,3,2,0:T(2,128)S(1)} %get-tuple-element.507), channel_id=1, source_target_pairs={{16,0},{32,16},{48,32},{64,48},{80,64},{96,80},{112,96},{128,112},... | collective-permute-start | bytes 55304 | tf_op jit(solution)/shard_map/while/body/eval_jaxpr/ppermute | solution.py:11
  65.2 1.9 collective-permute-start.1
  67.2 2.6 collective-permute-done.1
  69.9 9.8 %collective-permute-start = (f32[2,2,3,3,128]{4,1,3,2,0:T(2,128)S(1)}, f32[2,2,3,3,128]{4,1,3,2,0:T(2,128)S(1)}, u32[]{:S(2)}, u32[]{:S(2)}) collective-permute-start(f32[2,2,3,3,128]{4,1,3,2,0:T(2,128)S(1)} %get-tuple-element.507), channel_id=1, source_target_pairs={{16,0},{32,16},{48,32},{64,48},{80,64},{96,80},{112,96},{128,112},... | collective-permute-start | bytes 55304 | tf_op jit(solution)/shard_map/while/body/eval_jaxpr/ppermute | solution.py:11
  79.8 1.9 collective-permute-start.1
  81.7 2.6 collective-permute-done.1
  84.4 9.8 %collective-permute-start = (f32[2,2,3,3,128]{4,1,3,2,0:T(2,128)S(1)}, f32[2,2,3,3,128]{4,1,3,2,0:T(2,128)S(1)}, u32[]{:S(2)}, u32[]{:S(2)}) collective-permute-start(f32[2,2,3,3,128]{4,1,3,2,0:T(2,128)S(1)} %get-tuple-element.507), channel_id=1, source_target_pairs={{16,0},{32,16},{48,32},{64,48},{80,64},{96,80},{112,96},{128,112},... | collective-permute-start | bytes 55304 | tf_op jit(solution)/shard_map/while/body/eval_jaxpr/ppermute | solution.py:11
  94.3 1.9 collective-permute-start.1
  96.3 2.6 collective-permute-done.1
  99.0 9.8 %collective-permute-start = (f32[2,2,3,3,128]{4,1,3,2,0:T(2,128)S(1)}, f32[2,2,3,3,128]{4,1,3,2,0:T(2,128)S(1)}, u32[]{:S(2)}, u32[]{:S(2)}) collective-permute-start(f32[2,2,3,3,128]{4,1,3,2,0:T(2,128)S(1)} %get-tuple-element.507), channel_id=1, source_target_pairs={{16,0},{32,16},{48,32},{64,48},{80,64},{96,80},{112,96},{128,112},... | collective-permute-start | bytes 55304 | tf_op jit(solution)/shard_map/while/body/eval_jaxpr/ppermute | solution.py:11
  108.8 1.9 collective-permute-start.1
  110.8 2.6 collective-permute-done.1
  113.5 9.8 %collective-permute-start = (f32[2,2,3,3,128]{4,1,3,2,0:T(2,128)S(1)}, f32[2,2,3,3,128]{4,1,3,2,0:T(2,128)S(1)}, u32[]{:S(2)}, u32[]{:S(2)}) collective-permute-start(f32[2,2,3,3,128]{4,1,3,2,0:T(2,128)S(1)} %get-tuple-element.507), channel_id=1, source_target_pairs={{16,0},{32,16},{48,32},{64,48},{80,64},{96,80},{112,96},{128,112},... | collective-permute-start | bytes 55304 | tf_op jit(solution)/shard_map/while/body/eval_jaxpr/ppermute | solution.py:11
  123.3 1.9 collective-permute-start.1
  125.3 2.6 collective-permute-done.1
  128.0 9.8 %collective-permute-start = (f32[2,2,3,3,128]{4,1,3,2,0:T(2,128)S(1)}, f32[2,2,3,3,128]{4,1,3,2,0:T(2,128)S(1)}, u32[]{:S(2)}, u32[]{:S(2)}) collective-permute-start(f32[2,2,3,3,128]{4,1,3,2,0:T(2,128)S(1)} %get-tuple-element.507), channel_id=1, source_target_pairs={{16,0},{32,16},{48,32},{64,48},{80,64},{96,80},{112,96},{128,112},... | collective-permute-start | bytes 55304 | tf_op jit(solution)/shard_map/while/body/eval_jaxpr/ppermute | solution.py:11
  137.8 1.9 collective-permute-start.1
  139.8 2.6 collective-permute-done.1
  142.5 9.8 %collective-permute-start = (f32[2,2,3,3,128]{4,1,3,2,0:T(2,128)S(1)}, f32[2,2,3,3,128]{4,1,3,2,0:T(2,128)S(1)}, u32[]{:S(2)}, u32[]{:S(2)}) collective-permute-start(f32[2,2,3,3,128]{4,1,3,2,0:T(2,128)S(1)} %get-tuple-element.507), channel_id=1, source_target_pairs={{16,0},{32,16},{48,32},{64,48},{80,64},{96,80},{112,96},{128,112},... | collective-permute-start | bytes 55304 | tf_op jit(solution)/shard_map/while/body/eval_jaxpr/ppermute | solution.py:11
  152.3 1.9 collective-permute-start.1
  154.3 2.6 collective-permute-done.1
  157.0 9.8 %collective-permute-start = (f32[2,2,3,3,128]{4,1,3,2,0:T(2,128)S(1)}, f32[2,2,3,3,128]{4,1,3,2,0:T(2,128)S(1)}, u32[]{:S(2)}, u32[]{:S(2)}) collective-permute-start(f32[2,2,3,3,128]{4,1,3,2,0:T(2,128)S(1)} %get-tuple-element.507), channel_id=1, source_target_pairs={{16,0},{32,16},{48,32},{64,48},{80,64},{96,80},{112,96},{128,112},... | collective-permute-start | bytes 55304 | tf_op jit(solution)/shard_map/while/body/eval_jaxpr/ppermute | solution.py:11
  166.9 1.9 collective-permute-start.1
  168.9 2.6 collective-permute-done.1
  171.6 9.8 %collective-permute-start = (f32[2,2,3,3,128]{4,1,3,2,0:T(2,128)S(1)}, f32[2,2,3,3,128]{4,1,3,2,0:T(2,128)S(1)}, u32[]{:S(2)}, u32[]{:S(2)}) collective-permute-start(f32[2,2,3,3,128]{4,1,3,2,0:T(2,128)S(1)} %get-tuple-element.507), channel_id=1, source_target_pairs={{16,0},{32,16},{48,32},{64,48},{80,64},{96,80},{112,96},{128,112},... | collective-permute-start | bytes 55304 | tf_op jit(solution)/shard_map/while/body/eval_jaxpr/ppermute | solution.py:11
  181.4 1.9 collective-permute-start.1
  183.4 2.6 collective-permute-done.1
  189.8 184.4 %while.51 = (s32[]{:T(128)}, f32[2,2,3,3,128]{4,0,3,2,1:T(2,128)}, f32[24,8,2,2,3,3,128]{6,1,5,4,3,2,0:T(8,128)S(1)}, f32[24,2,2,3,3,128]{5,1,4,3,2,0:T(2,128)},...) while((s32[]{:T(128)}, f32[2,2,3,3,128]{4,0,3,2,1:T(2,128)}, ...), condition=%wide.region_15.16_spmd, body=%wide.region_2.15_spmd.sunk | while | flops 910086 | bytes 2968279 | solution.py:63
  374.2 2.1 copy.70
  376.3 2.0 reshape.184
  378.3 3.3 fusion.5
  382.8 3.8 multiply_reduce_fusion.27
  387.9 4.2 fusion.7
  392.1 100.0 %psum.7 = f32[64,192]{1,0:T(8,128)S(1)} all-reduce(f32[64,192]{1,0:T(8,128)} %fusion.7), channel_id=1, replica_groups=mesh['gx'=32,'yz'=16] {'gx','yz'}, use_global_device_ids=true, to_apply=%region_37.38 | all-reduce | flops 12288 | bytes 98304 | tf_op jit(solution)/shard_map/psum | solution.py:97
  493.3 4.7 fusion.6
  498.1 104.9 %while.52 = (s32[]{:T(128)}, f32[8,26,2,3,3,128]{5,0,4,3,2,1:T(8,128)S(1)}, s32[24]{0:T(128)S(1)}, f32[24,2,2,3,3,128]{5,1,4,3,2,0:T(2,128)}, f32[24,8,2,2,3,3,1...) while((s32[]{:T(128)}, f32[8,26,2,3,3,128]{5,0,4,3,2,1:T(8,128)S(1)}, s32[24]{0:T(128)S(1)}, ...), condition=%wide.region_34.35_spmd, body=%wide.region_25.34_spmd.sunk | while | flops 891653 | bytes 3411083 | solution.py:84
  604.4 2.9 rev.3
  607.3 161.5 %while.53 = (s32[]{:T(128)}, f32[8,2,2,3,3,128]{5,4,3,2,1,0:T(4,128)S(1)}, f32[12,8,2,2,3,3,128]{6,1,5,4,3,2,0:T(8,128)}, s32[]{:T(128)}) while((s32[]{:T(128)}, f32[8,2,2,3,3,128]{5,4,3,2,1,0:T(4,128)S(1)}, f32[12,8,2,2,3,3,128]{6,1,5,4,3,2,0:T(8,128)}, s32[]{:T(128)}) %tuple.163), condition=%wide.region_36.37_spmd, body=%wide.region_35.36_spmd.sunk | while | flops 36866 | bytes 1327209 | solution.py:93
  607.3 2.1 collective-permute-start.2
  610.3 12.3 %collective-permute-done.2 = f32[8,2,2,3,3,128]{5,4,3,2,1,0:T(4,128)S(1)} collective-permute-done((f32[8,2,2,3,3,128]{5,4,3,2,1,0:T(4,128)S(1)}, f32[8,2,2,3,3,128]{5,4,3,2,1,0:T(4,128)S(1)}, u32[]{:S(2)}, u32[]{:S(2)}) %collective-permute-start.2) | collective-permute-done | bytes 147488 | tf_op jit(solution)/shard_map/while/body/eval_jaxpr/ppermute | solution.py:11
  625.5 12.2 %collective-permute-done.2 = f32[8,2,2,3,3,128]{5,4,3,2,1,0:T(4,128)S(1)} collective-permute-done((f32[8,2,2,3,3,128]{5,4,3,2,1,0:T(4,128)S(1)}, f32[8,2,2,3,3,128]{5,4,3,2,1,0:T(4,128)S(1)}, u32[]{:S(2)}, u32[]{:S(2)}) %collective-permute-start.2) | collective-permute-done | bytes 147488 | tf_op jit(solution)/shard_map/while/body/eval_jaxpr/ppermute | solution.py:11
  640.7 10.2 %collective-permute-done.2 = f32[8,2,2,3,3,128]{5,4,3,2,1,0:T(4,128)S(1)} collective-permute-done((f32[8,2,2,3,3,128]{5,4,3,2,1,0:T(4,128)S(1)}, f32[8,2,2,3,3,128]{5,4,3,2,1,0:T(4,128)S(1)}, u32[]{:S(2)}, u32[]{:S(2)}) %collective-permute-start.2) | collective-permute-done | bytes 147488 | tf_op jit(solution)/shard_map/while/body/eval_jaxpr/ppermute | solution.py:11
  651.1 1.9 collective-permute-start.2
  653.9 10.2 %collective-permute-done.2 = f32[8,2,2,3,3,128]{5,4,3,2,1,0:T(4,128)S(1)} collective-permute-done((f32[8,2,2,3,3,128]{5,4,3,2,1,0:T(4,128)S(1)}, f32[8,2,2,3,3,128]{5,4,3,2,1,0:T(4,128)S(1)}, u32[]{:S(2)}, u32[]{:S(2)}) %collective-permute-start.2) | collective-permute-done | bytes 147488 | tf_op jit(solution)/shard_map/while/body/eval_jaxpr/ppermute | solution.py:11
  667.0 10.1 %collective-permute-done.2 = f32[8,2,2,3,3,128]{5,4,3,2,1,0:T(4,128)S(1)} collective-permute-done((f32[8,2,2,3,3,128]{5,4,3,2,1,0:T(4,128)S(1)}, f32[8,2,2,3,3,128]{5,4,3,2,1,0:T(4,128)S(1)}, u32[]{:S(2)}, u32[]{:S(2)}) %collective-permute-start.2) | collective-permute-done | bytes 147488 | tf_op jit(solution)/shard_map/while/body/eval_jaxpr/ppermute | solution.py:11
  677.2 1.9 collective-permute-start.2
  680.1 10.1 %collective-permute-done.2 = f32[8,2,2,3,3,128]{5,4,3,2,1,0:T(4,128)S(1)} collective-permute-done((f32[8,2,2,3,3,128]{5,4,3,2,1,0:T(4,128)S(1)}, f32[8,2,2,3,3,128]{5,4,3,2,1,0:T(4,128)S(1)}, u32[]{:S(2)}, u32[]{:S(2)}) %collective-permute-start.2) | collective-permute-done | bytes 147488 | tf_op jit(solution)/shard_map/while/body/eval_jaxpr/ppermute | solution.py:11
  693.2 10.1 %collective-permute-done.2 = f32[8,2,2,3,3,128]{5,4,3,2,1,0:T(4,128)S(1)} collective-permute-done((f32[8,2,2,3,3,128]{5,4,3,2,1,0:T(4,128)S(1)}, f32[8,2,2,3,3,128]{5,4,3,2,1,0:T(4,128)S(1)}, u32[]{:S(2)}, u32[]{:S(2)}) %collective-permute-start.2) | collective-permute-done | bytes 147488 | tf_op jit(solution)/shard_map/while/body/eval_jaxpr/ppermute | solution.py:11
  706.3 10.1 %collective-permute-done.2 = f32[8,2,2,3,3,128]{5,4,3,2,1,0:T(4,128)S(1)} collective-permute-done((f32[8,2,2,3,3,128]{5,4,3,2,1,0:T(4,128)S(1)}, f32[8,2,2,3,3,128]{5,4,3,2,1,0:T(4,128)S(1)}, u32[]{:S(2)}, u32[]{:S(2)}) %collective-permute-start.2) | collective-permute-done | bytes 147488 | tf_op jit(solution)/shard_map/while/body/eval_jaxpr/ppermute | solution.py:11
  719.4 10.1 %collective-permute-done.2 = f32[8,2,2,3,3,128]{5,4,3,2,1,0:T(4,128)S(1)} collective-permute-done((f32[8,2,2,3,3,128]{5,4,3,2,1,0:T(4,128)S(1)}, f32[8,2,2,3,3,128]{5,4,3,2,1,0:T(4,128)S(1)}, u32[]{:S(2)}, u32[]{:S(2)}) %collective-permute-start.2) | collective-permute-done | bytes 147488 | tf_op jit(solution)/shard_map/while/body/eval_jaxpr/ppermute | solution.py:11
  729.6 1.9 collective-permute-start.2
  732.5 10.1 %collective-permute-done.2 = f32[8,2,2,3,3,128]{5,4,3,2,1,0:T(4,128)S(1)} collective-permute-done((f32[8,2,2,3,3,128]{5,4,3,2,1,0:T(4,128)S(1)}, f32[8,2,2,3,3,128]{5,4,3,2,1,0:T(4,128)S(1)}, u32[]{:S(2)}, u32[]{:S(2)}) %collective-permute-start.2) | collective-permute-done | bytes 147488 | tf_op jit(solution)/shard_map/while/body/eval_jaxpr/ppermute | solution.py:11
  745.6 10.1 %collective-permute-done.2 = f32[8,2,2,3,3,128]{5,4,3,2,1,0:T(4,128)S(1)} collective-permute-done((f32[8,2,2,3,3,128]{5,4,3,2,1,0:T(4,128)S(1)}, f32[8,2,2,3,3,128]{5,4,3,2,1,0:T(4,128)S(1)}, u32[]{:S(2)}, u32[]{:S(2)}) %collective-permute-start.2) | collective-permute-done | bytes 147488 | tf_op jit(solution)/shard_map/while/body/eval_jaxpr/ppermute | solution.py:11
  758.7 10.1 %collective-permute-done.2 = f32[8,2,2,3,3,128]{5,4,3,2,1,0:T(4,128)S(1)} collective-permute-done((f32[8,2,2,3,3,128]{5,4,3,2,1,0:T(4,128)S(1)}, f32[8,2,2,3,3,128]{5,4,3,2,1,0:T(4,128)S(1)}, u32[]{:S(2)}, u32[]{:S(2)}) %collective-permute-start.2) | collective-permute-done | bytes 147488 | tf_op jit(solution)/shard_map/while/body/eval_jaxpr/ppermute | solution.py:11
  (1181 shorter events, 234.8 us)
Async XLA Ops:
  1.6 184.5 %copy-start.11 = (f32[2,2,3,3,128]{4,1,3,2,0:T(2,128)S(1)}, f32[2,2,3,3,128]{4,1,3,2,0:T(2,128)}, u32[]{:S(2)}) copy-start(f32[2,2,3,3,128]{4,1,3,2,0:T(2,128)} %param.12) | copy-start | bytes 55300
  2.4 18.2 %collective-permute-start = (f32[2,2,3,3,128]{4,1,3,2,0:T(2,128)S(1)}, f32[2,2,3,3,128]{4,1,3,2,0:T(2,128)S(1)}, u32[]{:S(2)}, u32[]{:S(2)}) collective-permute-start(f32[2,2,3,3,128]{4,1,3,2,0:T(2,128)S(1)} %get-tuple-element.507), channel_id=1, source_target_pairs={{16,0},{32,16},{48,32},{64,48},{80,64},{96,80},{112,96},{128,112},... | collective-permute-start | bytes 55304 | tf_op jit(solution)/shard_map/while/body/eval_jaxpr/ppermute | solution.py:11
  18.0 6.8 collective-permute-start.1
  24.9 11.7 %collective-permute-start = (f32[2,2,3,3,128]{4,1,3,2,0:T(2,128)S(1)}, f32[2,2,3,3,128]{4,1,3,2,0:T(2,128)S(1)}, u32[]{:S(2)}, u32[]{:S(2)}) collective-permute-start(f32[2,2,3,3,128]{4,1,3,2,0:T(2,128)S(1)} %get-tuple-element.507), channel_id=1, source_target_pairs={{16,0},{32,16},{48,32},{64,48},{80,64},{96,80},{112,96},{128,112},... | collective-permute-start | bytes 55304 | tf_op jit(solution)/shard_map/while/body/eval_jaxpr/ppermute | solution.py:11
  34.7 5.9 collective-permute-start.1
  40.8 11.8 %collective-permute-start = (f32[2,2,3,3,128]{4,1,3,2,0:T(2,128)S(1)}, f32[2,2,3,3,128]{4,1,3,2,0:T(2,128)S(1)}, u32[]{:S(2)}, u32[]{:S(2)}) collective-permute-start(f32[2,2,3,3,128]{4,1,3,2,0:T(2,128)S(1)} %get-tuple-element.507), channel_id=1, source_target_pairs={{16,0},{32,16},{48,32},{64,48},{80,64},{96,80},{112,96},{128,112},... | collective-permute-start | bytes 55304 | tf_op jit(solution)/shard_map/while/body/eval_jaxpr/ppermute | solution.py:11
  50.6 4.7 collective-permute-start.1
  55.4 11.8 %collective-permute-start = (f32[2,2,3,3,128]{4,1,3,2,0:T(2,128)S(1)}, f32[2,2,3,3,128]{4,1,3,2,0:T(2,128)S(1)}, u32[]{:S(2)}, u32[]{:S(2)}) collective-permute-start(f32[2,2,3,3,128]{4,1,3,2,0:T(2,128)S(1)} %get-tuple-element.507), channel_id=1, source_target_pairs={{16,0},{32,16},{48,32},{64,48},{80,64},{96,80},{112,96},{128,112},... | collective-permute-start | bytes 55304 | tf_op jit(solution)/shard_map/while/body/eval_jaxpr/ppermute | solution.py:11
  65.2 4.6 collective-permute-start.1
  69.9 11.8 %collective-permute-start = (f32[2,2,3,3,128]{4,1,3,2,0:T(2,128)S(1)}, f32[2,2,3,3,128]{4,1,3,2,0:T(2,128)S(1)}, u32[]{:S(2)}, u32[]{:S(2)}) collective-permute-start(f32[2,2,3,3,128]{4,1,3,2,0:T(2,128)S(1)} %get-tuple-element.507), channel_id=1, source_target_pairs={{16,0},{32,16},{48,32},{64,48},{80,64},{96,80},{112,96},{128,112},... | collective-permute-start | bytes 55304 | tf_op jit(solution)/shard_map/while/body/eval_jaxpr/ppermute | solution.py:11
  79.8 4.6 collective-permute-start.1
  84.4 11.8 %collective-permute-start = (f32[2,2,3,3,128]{4,1,3,2,0:T(2,128)S(1)}, f32[2,2,3,3,128]{4,1,3,2,0:T(2,128)S(1)}, u32[]{:S(2)}, u32[]{:S(2)}) collective-permute-start(f32[2,2,3,3,128]{4,1,3,2,0:T(2,128)S(1)} %get-tuple-element.507), channel_id=1, source_target_pairs={{16,0},{32,16},{48,32},{64,48},{80,64},{96,80},{112,96},{128,112},... | collective-permute-start | bytes 55304 | tf_op jit(solution)/shard_map/while/body/eval_jaxpr/ppermute | solution.py:11
  94.3 4.6 collective-permute-start.1
  99.0 11.8 %collective-permute-start = (f32[2,2,3,3,128]{4,1,3,2,0:T(2,128)S(1)}, f32[2,2,3,3,128]{4,1,3,2,0:T(2,128)S(1)}, u32[]{:S(2)}, u32[]{:S(2)}) collective-permute-start(f32[2,2,3,3,128]{4,1,3,2,0:T(2,128)S(1)} %get-tuple-element.507), channel_id=1, source_target_pairs={{16,0},{32,16},{48,32},{64,48},{80,64},{96,80},{112,96},{128,112},... | collective-permute-start | bytes 55304 | tf_op jit(solution)/shard_map/while/body/eval_jaxpr/ppermute | solution.py:11
  108.8 4.6 collective-permute-start.1
  113.5 11.8 %collective-permute-start = (f32[2,2,3,3,128]{4,1,3,2,0:T(2,128)S(1)}, f32[2,2,3,3,128]{4,1,3,2,0:T(2,128)S(1)}, u32[]{:S(2)}, u32[]{:S(2)}) collective-permute-start(f32[2,2,3,3,128]{4,1,3,2,0:T(2,128)S(1)} %get-tuple-element.507), channel_id=1, source_target_pairs={{16,0},{32,16},{48,32},{64,48},{80,64},{96,80},{112,96},{128,112},... | collective-permute-start | bytes 55304 | tf_op jit(solution)/shard_map/while/body/eval_jaxpr/ppermute | solution.py:11
  123.3 4.6 collective-permute-start.1
  128.0 11.8 %collective-permute-start = (f32[2,2,3,3,128]{4,1,3,2,0:T(2,128)S(1)}, f32[2,2,3,3,128]{4,1,3,2,0:T(2,128)S(1)}, u32[]{:S(2)}, u32[]{:S(2)}) collective-permute-start(f32[2,2,3,3,128]{4,1,3,2,0:T(2,128)S(1)} %get-tuple-element.507), channel_id=1, source_target_pairs={{16,0},{32,16},{48,32},{64,48},{80,64},{96,80},{112,96},{128,112},... | collective-permute-start | bytes 55304 | tf_op jit(solution)/shard_map/while/body/eval_jaxpr/ppermute | solution.py:11
  137.8 4.6 collective-permute-start.1
  142.5 11.8 %collective-permute-start = (f32[2,2,3,3,128]{4,1,3,2,0:T(2,128)S(1)}, f32[2,2,3,3,128]{4,1,3,2,0:T(2,128)S(1)}, u32[]{:S(2)}, u32[]{:S(2)}) collective-permute-start(f32[2,2,3,3,128]{4,1,3,2,0:T(2,128)S(1)} %get-tuple-element.507), channel_id=1, source_target_pairs={{16,0},{32,16},{48,32},{64,48},{80,64},{96,80},{112,96},{128,112},... | collective-permute-start | bytes 55304 | tf_op jit(solution)/shard_map/while/body/eval_jaxpr/ppermute | solution.py:11
  152.3 4.6 collective-permute-start.1
  157.0 11.8 %collective-permute-start = (f32[2,2,3,3,128]{4,1,3,2,0:T(2,128)S(1)}, f32[2,2,3,3,128]{4,1,3,2,0:T(2,128)S(1)}, u32[]{:S(2)}, u32[]{:S(2)}) collective-permute-start(f32[2,2,3,3,128]{4,1,3,2,0:T(2,128)S(1)} %get-tuple-element.507), channel_id=1, source_target_pairs={{16,0},{32,16},{48,32},{64,48},{80,64},{96,80},{112,96},{128,112},... | collective-permute-start | bytes 55304 | tf_op jit(solution)/shard_map/while/body/eval_jaxpr/ppermute | solution.py:11
  166.9 4.6 collective-permute-start.1
  171.6 11.8 %collective-permute-start = (f32[2,2,3,3,128]{4,1,3,2,0:T(2,128)S(1)}, f32[2,2,3,3,128]{4,1,3,2,0:T(2,128)S(1)}, u32[]{:S(2)}, u32[]{:S(2)}) collective-permute-start(f32[2,2,3,3,128]{4,1,3,2,0:T(2,128)S(1)} %get-tuple-element.507), channel_id=1, source_target_pairs={{16,0},{32,16},{48,32},{64,48},{80,64},{96,80},{112,96},{128,112},... | collective-permute-start | bytes 55304 | tf_op jit(solution)/shard_map/while/body/eval_jaxpr/ppermute | solution.py:11
  181.4 4.6 collective-permute-start.1
  192.5 2.7 copy-start.3
  200.2 2.7 copy-start.3
  207.9 2.7 copy-start.3
  215.6 2.7 copy-start.3
  223.2 2.7 copy-start.3
  230.9 2.7 copy-start.3
  238.6 2.7 copy-start.3
  246.3 2.7 copy-start.3
  254.0 2.7 copy-start.3
  261.7 2.7 copy-start.3
  269.4 2.7 copy-start.3
  277.1 2.7 copy-start.3
  284.8 2.7 copy-start.3
  292.4 2.7 copy-start.3
  300.1 2.7 copy-start.3
  307.8 2.7 copy-start.3
  315.5 2.7 copy-start.3
  323.2 2.7 copy-start.3
  330.9 2.7 copy-start.3
  338.6 2.7 copy-start.3
  346.3 2.7 copy-start.3
  353.9 2.7 copy-start.3
  392.1 101.2 %copy-start.1 = (f32[8,8,2,2,3,3,128]{6,1,5,4,3,2,0:T(8,128)S(1)}, f32[8,8,2,2,3,3,128]{6,1,5,4,3,2,0:T(8,128)}, u32[]{:S(2)}) copy-start(f32[8,8,2,2,3,3,128]{6,1,5,4,3,2,0:T(8,128)} %copy-done) | copy-start | bytes 3538948
  392.1 101.2 %copy-start.9 = (f32[64,192]{1,0:T(8,128)S(1)}, f32[64,192]{1,0:T(8,128)}, u32[]{:S(2)}) copy-start(f32[64,192]{1,0:T(8,128)} %reshape.184) | copy-start | bytes 147460
  604.4 164.5 %copy-start.6 = (f32[8,8,2,3,3,128]{5,1,4,3,2,0:T(8,128)S(1)}, f32[8,8,2,3,3,128]{5,1,4,3,2,0:T(8,128)}, u32[]{:S(2)}) copy-start(f32[8,8,2,3,3,128]{5,1,4,3,2,0:T(8,128)} %get-tuple-element.198) | copy-start | bytes 1769476
  607.2 161.6 %copy-start.5 = (f32[8,8,2,3,3,128]{5,1,4,3,2,0:T(8,128)S(1)}, f32[8,8,2,3,3,128]{5,1,4,3,2,0:T(8,128)}, u32[]{:S(2)}) copy-start(f32[8,8,2,3,3,128]{5,1,4,3,2,0:T(8,128)} %get-tuple-element.197) | copy-start | bytes 1769476
  607.3 161.6 %copy-start.4 = (f32[8,8,2,3,3,128]{5,1,4,3,2,0:T(8,128)S(1)}, f32[8,8,2,3,3,128]{5,1,4,3,2,0:T(8,128)}, u32[]{:S(2)}) copy-start(f32[8,8,2,3,3,128]{5,1,4,3,2,0:T(8,128)} %get-tuple-element.196) | copy-start | bytes 1769476
  607.3 15.2 %collective-permute-start.2 = (f32[8,2,2,3,3,128]{5,4,3,2,1,0:T(4,128)S(1)}, f32[8,2,2,3,3,128]{5,4,3,2,1,0:T(4,128)S(1)}, u32[]{:S(2)}, u32[]{:S(2)}) collective-permute-start(f32[8,2,2,3,3,128]{5,4,3,2,1,0:T(4,128)S(1)} %get-tuple-element.580), channel_id=1, source_target_pairs={{496,0},{0,16},{16,32},{32,48},{48,64},{64,80},{80,96},{96,112},{1... | collective-permute-start | bytes 442376 | tf_op jit(solution)/shard_map/while/body/eval_jaxpr/ppermute | solution.py:11
  622.7 15.1 %collective-permute-start.2 = (f32[8,2,2,3,3,128]{5,4,3,2,1,0:T(4,128)S(1)}, f32[8,2,2,3,3,128]{5,4,3,2,1,0:T(4,128)S(1)}, u32[]{:S(2)}, u32[]{:S(2)}) collective-permute-start(f32[8,2,2,3,3,128]{5,4,3,2,1,0:T(4,128)S(1)} %get-tuple-element.580), channel_id=1, source_target_pairs={{496,0},{0,16},{16,32},{32,48},{48,64},{64,80},{80,96},{96,112},{1... | collective-permute-start | bytes 442376 | tf_op jit(solution)/shard_map/while/body/eval_jaxpr/ppermute | solution.py:11
  637.9 13.1 %collective-permute-start.2 = (f32[8,2,2,3,3,128]{5,4,3,2,1,0:T(4,128)S(1)}, f32[8,2,2,3,3,128]{5,4,3,2,1,0:T(4,128)S(1)}, u32[]{:S(2)}, u32[]{:S(2)}) collective-permute-start(f32[8,2,2,3,3,128]{5,4,3,2,1,0:T(4,128)S(1)} %get-tuple-element.580), channel_id=1, source_target_pairs={{496,0},{0,16},{16,32},{32,48},{48,64},{64,80},{80,96},{96,112},{1... | collective-permute-start | bytes 442376 | tf_op jit(solution)/shard_map/while/body/eval_jaxpr/ppermute | solution.py:11
  651.1 13.0 %collective-permute-start.2 = (f32[8,2,2,3,3,128]{5,4,3,2,1,0:T(4,128)S(1)}, f32[8,2,2,3,3,128]{5,4,3,2,1,0:T(4,128)S(1)}, u32[]{:S(2)}, u32[]{:S(2)}) collective-permute-start(f32[8,2,2,3,3,128]{5,4,3,2,1,0:T(4,128)S(1)} %get-tuple-element.580), channel_id=1, source_target_pairs={{496,0},{0,16},{16,32},{32,48},{48,64},{64,80},{80,96},{96,112},{1... | collective-permute-start | bytes 442376 | tf_op jit(solution)/shard_map/while/body/eval_jaxpr/ppermute | solution.py:11
  664.2 13.0 %collective-permute-start.2 = (f32[8,2,2,3,3,128]{5,4,3,2,1,0:T(4,128)S(1)}, f32[8,2,2,3,3,128]{5,4,3,2,1,0:T(4,128)S(1)}, u32[]{:S(2)}, u32[]{:S(2)}) collective-permute-start(f32[8,2,2,3,3,128]{5,4,3,2,1,0:T(4,128)S(1)} %get-tuple-element.580), channel_id=1, source_target_pairs={{496,0},{0,16},{16,32},{32,48},{48,64},{64,80},{80,96},{96,112},{1... | collective-permute-start | bytes 442376 | tf_op jit(solution)/shard_map/while/body/eval_jaxpr/ppermute | solution.py:11
  677.2 13.0 %collective-permute-start.2 = (f32[8,2,2,3,3,128]{5,4,3,2,1,0:T(4,128)S(1)}, f32[8,2,2,3,3,128]{5,4,3,2,1,0:T(4,128)S(1)}, u32[]{:S(2)}, u32[]{:S(2)}) collective-permute-start(f32[8,2,2,3,3,128]{5,4,3,2,1,0:T(4,128)S(1)} %get-tuple-element.580), channel_id=1, source_target_pairs={{496,0},{0,16},{16,32},{32,48},{48,64},{64,80},{80,96},{96,112},{1... | collective-permute-start | bytes 442376 | tf_op jit(solution)/shard_map/while/body/eval_jaxpr/ppermute | solution.py:11
  690.3 13.0 %collective-permute-start.2 = (f32[8,2,2,3,3,128]{5,4,3,2,1,0:T(4,128)S(1)}, f32[8,2,2,3,3,128]{5,4,3,2,1,0:T(4,128)S(1)}, u32[]{:S(2)}, u32[]{:S(2)}) collective-permute-start(f32[8,2,2,3,3,128]{5,4,3,2,1,0:T(4,128)S(1)} %get-tuple-element.580), channel_id=1, source_target_pairs={{496,0},{0,16},{16,32},{32,48},{48,64},{64,80},{80,96},{96,112},{1... | collective-permute-start | bytes 442376 | tf_op jit(solution)/shard_map/while/body/eval_jaxpr/ppermute | solution.py:11
  703.4 13.0 %collective-permute-start.2 = (f32[8,2,2,3,3,128]{5,4,3,2,1,0:T(4,128)S(1)}, f32[8,2,2,3,3,128]{5,4,3,2,1,0:T(4,128)S(1)}, u32[]{:S(2)}, u32[]{:S(2)}) collective-permute-start(f32[8,2,2,3,3,128]{5,4,3,2,1,0:T(4,128)S(1)} %get-tuple-element.580), channel_id=1, source_target_pairs={{496,0},{0,16},{16,32},{32,48},{48,64},{64,80},{80,96},{96,112},{1... | collective-permute-start | bytes 442376 | tf_op jit(solution)/shard_map/while/body/eval_jaxpr/ppermute | solution.py:11
  716.5 13.0 %collective-permute-start.2 = (f32[8,2,2,3,3,128]{5,4,3,2,1,0:T(4,128)S(1)}, f32[8,2,2,3,3,128]{5,4,3,2,1,0:T(4,128)S(1)}, u32[]{:S(2)}, u32[]{:S(2)}) collective-permute-start(f32[8,2,2,3,3,128]{5,4,3,2,1,0:T(4,128)S(1)} %get-tuple-element.580), channel_id=1, source_target_pairs={{496,0},{0,16},{16,32},{32,48},{48,64},{64,80},{80,96},{96,112},{1... | collective-permute-start | bytes 442376 | tf_op jit(solution)/shard_map/while/body/eval_jaxpr/ppermute | solution.py:11
  729.6 13.0 %collective-permute-start.2 = (f32[8,2,2,3,3,128]{5,4,3,2,1,0:T(4,128)S(1)}, f32[8,2,2,3,3,128]{5,4,3,2,1,0:T(4,128)S(1)}, u32[]{:S(2)}, u32[]{:S(2)}) collective-permute-start(f32[8,2,2,3,3,128]{5,4,3,2,1,0:T(4,128)S(1)} %get-tuple-element.580), channel_id=1, source_target_pairs={{496,0},{0,16},{16,32},{32,48},{48,64},{64,80},{80,96},{96,112},{1... | collective-permute-start | bytes 442376 | tf_op jit(solution)/shard_map/while/body/eval_jaxpr/ppermute | solution.py:11
  742.7 13.0 %collective-permute-start.2 = (f32[8,2,2,3,3,128]{5,4,3,2,1,0:T(4,128)S(1)}, f32[8,2,2,3,3,128]{5,4,3,2,1,0:T(4,128)S(1)}, u32[]{:S(2)}, u32[]{:S(2)}) collective-permute-start(f32[8,2,2,3,3,128]{5,4,3,2,1,0:T(4,128)S(1)} %get-tuple-element.580), channel_id=1, source_target_pairs={{496,0},{0,16},{16,32},{32,48},{48,64},{64,80},{80,96},{96,112},{1... | collective-permute-start | bytes 442376 | tf_op jit(solution)/shard_map/while/body/eval_jaxpr/ppermute | solution.py:11
  755.8 13.0 %collective-permute-start.2 = (f32[8,2,2,3,3,128]{5,4,3,2,1,0:T(4,128)S(1)}, f32[8,2,2,3,3,128]{5,4,3,2,1,0:T(4,128)S(1)}, u32[]{:S(2)}, u32[]{:S(2)}) collective-permute-start(f32[8,2,2,3,3,128]{5,4,3,2,1,0:T(4,128)S(1)} %get-tuple-element.580), channel_id=1, source_target_pairs={{496,0},{0,16},{16,32},{32,48},{48,64},{64,80},{80,96},{96,112},{1... | collective-permute-start | bytes 442376 | tf_op jit(solution)/shard_map/while/body/eval_jaxpr/ppermute | solution.py:11
  (7 other events, 9.9 us)
where the time goes:
time: 780 us; the launch traced here: 771 us
  local copies, waits for them, and re-layouts  177 us (23%)
  starting transfers between devices  171 us (22%)
  waiting for transfers between devices  160 us (21%)
  blocking collectives  100 us (13%)
  loops' own time  96.8 us (12%)
  other arithmetic  53.1 us (7%)
  matrix products  12.2 us (2%)
    ppermute x36, starting transfers between devices, from_behind(): return lax.ppermute(block, axis, route)  171 us
    ppermute x36, waiting for transfers between devices, from_behind(): return lax.ppermute(block, axis, route)  160 us
    psum x1, blocking collectives, per_device(): summed = lax.psum(partial_grad, ('gx', 'yz'))  100 us
    mul x364, local copies, waits for them, and re-layouts, matmul_three(): left[..., :, :, None, :] * right[..., None, :, :, :]  64.4 us
    another operation x1, loops' own time, per_device(): lax.scan(forward_step, gauge_links, offsets)  51.7 us
    another operation x1, loops' own time, per_device(): lax.scan(backward_step, accumulator, (offsets, line_grad, all_lines))  44 us
    dynamic_slice x48, local copies, waits for them, and re-layouts, per_device(): lax.scan(forward_step, gauge_links, offsets)  29.5 us
    squeeze x24, local copies, waits for them, and re-layouts, per_device(): lax.scan(backward_step, accumulator, (offsets, line_grad, all_lines))  22.2 us
  transfers between devices with their start and end apart: 36, of which 24 were waited for; matrix products, arithmetic and copies ran while one was open for 1% of the time, Pallas kernels for 0%

commit v1 on v0

--- a/solution.py
+++ b/solution.py
@@ -94,7 +94,7 @@
     grad_field = direct + far_terms
     total_x = part_x * lax.axis_size("gx")
     total_sites = site_count * lax.axis_size("yz")
-    summed = lax.psum(partial_grad, ("gx", "yz"))
+    summed = lax.psum(lax.psum(partial_grad, "yz"), "gx")
     grad_weights = summed.reshape(channels, channels, line_count, channels) / math.sqrt(
         100.0 * total_x * total_sites
     )

time: 780 us -> 919 us (1.18)
  the two profiles are of different devices: /device:TPU:2 before, /device:TPU:32 now
where the time goes in v1:
time: 919 us; the launch traced here: 910 us
  blocking collectives  250 us (27%)
  local copies, waits for them, and re-layouts  177 us (19%)
  starting transfers between devices  165 us (18%)
  waiting for transfers between devices  155 us (17%)
  loops' own time  96.8 us (11%)
  other arithmetic  53.1 us (6%)
  matrix products  12.2 us (1%)
    psum x2, blocking collectives, per_device(): summed = lax.psum(lax.psum(partial_grad, 'yz'), 'gx')  250 us
    ppermute x36, starting transfers between devices, from_behind(): return lax.ppermute(block, axis, route)  165 us
    ppermute x36, waiting for transfers between devices, from_behind(): return lax.ppermute(block, axis, route)  155 us
    mul x364, local copies, waits for them, and re-layouts, matmul_three(): left[..., :, :, None, :] * right[..., None, :, :, :]  64.4 us
    another operation x1, loops' own time, per_device(): lax.scan(forward_step, gauge_links, offsets)  51.7 us
    another operation x1, loops' own time, per_device(): lax.scan(backward_step, accumulator, (offsets, line_grad, all_lines))  44 us
    dynamic_slice x48, local copies, waits for them, and re-layouts, per_device(): lax.scan(forward_step, gauge_links, offsets)  29.5 us
    squeeze x24, local copies, waits for them, and re-layouts, per_device(): lax.scan(backward_step, accumulator, (offsets, line_grad, all_lines))  22.2 us
  transfers between devices with their start and end apart: 36, of which 24 were waited for; matrix products, arithmetic and copies ran while one was open for 1% of the time, Pallas kernels for 0%

profile of v1, /device:TPU:32, one launch (start us, length us, event | category | flops | bytes accessed | tf_op | source)
XLA Modules:
  0.0 910.1 jit_solution(8239738062650898560)
XLA Ops:
  2.4 175.2 %while.50 = (s32[]{:T(128)}, f32[2,2,3,3,128]{4,1,3,2,0:T(2,128)S(1)}, f32[8,2,2,3,3,128]{5,2,4,3,1,0:T(2,128)S(1)}, f32[12,2,2,3,3,128]{5,1,0,4,3,2:T(2,128)S(1...) while((s32[]{:T(128)}, f32[2,2,3,3,128]{4,1,3,2,0:T(2,128)S(1)}, ...), condition=%wide.region_1.2_spmd, body=%wide.region_0.1_spmd.sunk | while | flops 2 | bytes 1327269 | solution.py:46
  2.4 9.9 %collective-permute-start = (f32[2,2,3,3,128]{4,1,3,2,0:T(2,128)S(1)}, f32[2,2,3,3,128]{4,1,3,2,0:T(2,128)S(1)}, u32[]{:S(2)}, u32[]{:S(2)}) collective-permute-start(f32[2,2,3,3,128]{4,1,3,2,0:T(2,128)S(1)} %get-tuple-element.507), channel_id=1, source_target_pairs={{16,0},{32,16},{48,32},{64,48},{80,64},{96,80},{112,96},{128,112},... | collective-permute-start | bytes 55304 | tf_op jit(solution)/shard_map/while/body/eval_jaxpr/ppermute | solution.py:11
  12.3 2.6 collective-permute-start.1
  14.9 2.8 collective-permute-done.1
  17.9 9.8 %collective-permute-start = (f32[2,2,3,3,128]{4,1,3,2,0:T(2,128)S(1)}, f32[2,2,3,3,128]{4,1,3,2,0:T(2,128)S(1)}, u32[]{:S(2)}, u32[]{:S(2)}) collective-permute-start(f32[2,2,3,3,128]{4,1,3,2,0:T(2,128)S(1)} %get-tuple-element.507), channel_id=1, source_target_pairs={{16,0},{32,16},{48,32},{64,48},{80,64},{96,80},{112,96},{128,112},... | collective-permute-start | bytes 55304 | tf_op jit(solution)/shard_map/while/body/eval_jaxpr/ppermute | solution.py:11
  27.7 1.9 collective-permute-start.1
  29.6 2.6 collective-permute-done.1
  32.4 9.8 %collective-permute-start = (f32[2,2,3,3,128]{4,1,3,2,0:T(2,128)S(1)}, f32[2,2,3,3,128]{4,1,3,2,0:T(2,128)S(1)}, u32[]{:S(2)}, u32[]{:S(2)}) collective-permute-start(f32[2,2,3,3,128]{4,1,3,2,0:T(2,128)S(1)} %get-tuple-element.507), channel_id=1, source_target_pairs={{16,0},{32,16},{48,32},{64,48},{80,64},{96,80},{112,96},{128,112},... | collective-permute-start | bytes 55304 | tf_op jit(solution)/shard_map/while/body/eval_jaxpr/ppermute | solution.py:11
  42.2 1.9 collective-permute-start.1
  44.2 2.6 collective-permute-done.1
  46.9 9.8 %collective-permute-start = (f32[2,2,3,3,128]{4,1,3,2,0:T(2,128)S(1)}, f32[2,2,3,3,128]{4,1,3,2,0:T(2,128)S(1)}, u32[]{:S(2)}, u32[]{:S(2)}) collective-permute-start(f32[2,2,3,3,128]{4,1,3,2,0:T(2,128)S(1)} %get-tuple-element.507), channel_id=1, source_target_pairs={{16,0},{32,16},{48,32},{64,48},{80,64},{96,80},{112,96},{128,112},... | collective-permute-start | bytes 55304 | tf_op jit(solution)/shard_map/while/body/eval_jaxpr/ppermute | solution.py:11
  56.7 1.9 collective-permute-start.1
  58.7 2.6 collective-permute-done.1
  61.4 9.8 %collective-permute-start = (f32[2,2,3,3,128]{4,1,3,2,0:T(2,128)S(1)}, f32[2,2,3,3,128]{4,1,3,2,0:T(2,128)S(1)}, u32[]{:S(2)}, u32[]{:S(2)}) collective-permute-start(f32[2,2,3,3,128]{4,1,3,2,0:T(2,128)S(1)} %get-tuple-element.507), channel_id=1, source_target_pairs={{16,0},{32,16},{48,32},{64,48},{80,64},{96,80},{112,96},{128,112},... | collective-permute-start | bytes 55304 | tf_op jit(solution)/shard_map/while/body/eval_jaxpr/ppermute | solution.py:11
  71.2 1.9 collective-permute-start.1
  73.2 2.6 collective-permute-done.1
  75.9 9.8 %collective-permute-start = (f32[2,2,3,3,128]{4,1,3,2,0:T(2,128)S(1)}, f32[2,2,3,3,128]{4,1,3,2,0:T(2,128)S(1)}, u32[]{:S(2)}, u32[]{:S(2)}) collective-permute-start(f32[2,2,3,3,128]{4,1,3,2,0:T(2,128)S(1)} %get-tuple-element.507), channel_id=1, source_target_pairs={{16,0},{32,16},{48,32},{64,48},{80,64},{96,80},{112,96},{128,112},... | collective-permute-start | bytes 55304 | tf_op jit(solution)/shard_map/while/body/eval_jaxpr/ppermute | solution.py:11
  85.8 1.9 collective-permute-start.1
  87.7 2.6 collective-permute-done.1
  90.5 9.8 %collective-permute-start = (f32[2,2,3,3,128]{4,1,3,2,0:T(2,128)S(1)}, f32[2,2,3,3,128]{4,1,3,2,0:T(2,128)S(1)}, u32[]{:S(2)}, u32[]{:S(2)}) collective-permute-start(f32[2,2,3,3,128]{4,1,3,2,0:T(2,128)S(1)} %get-tuple-element.507), channel_id=1, source_target_pairs={{16,0},{32,16},{48,32},{64,48},{80,64},{96,80},{112,96},{128,112},... | collective-permute-start | bytes 55304 | tf_op jit(solution)/shard_map/while/body/eval_jaxpr/ppermute | solution.py:11
  100.3 1.9 collective-permute-start.1
  102.3 2.6 collective-permute-done.1
  105.0 9.8 %collective-permute-start = (f32[2,2,3,3,128]{4,1,3,2,0:T(2,128)S(1)}, f32[2,2,3,3,128]{4,1,3,2,0:T(2,128)S(1)}, u32[]{:S(2)}, u32[]{:S(2)}) collective-permute-start(f32[2,2,3,3,128]{4,1,3,2,0:T(2,128)S(1)} %get-tuple-element.507), channel_id=1, source_target_pairs={{16,0},{32,16},{48,32},{64,48},{80,64},{96,80},{112,96},{128,112},... | collective-permute-start | bytes 55304 | tf_op jit(solution)/shard_map/while/body/eval_jaxpr/ppermute | solution.py:11
  116.8 2.6 collective-permute-done.1
  119.5 9.8 %collective-permute-start = (f32[2,2,3,3,128]{4,1,3,2,0:T(2,128)S(1)}, f32[2,2,3,3,128]{4,1,3,2,0:T(2,128)S(1)}, u32[]{:S(2)}, u32[]{:S(2)}) collective-permute-start(f32[2,2,3,3,128]{4,1,3,2,0:T(2,128)S(1)} %get-tuple-element.507), channel_id=1, source_target_pairs={{16,0},{32,16},{48,32},{64,48},{80,64},{96,80},{112,96},{128,112},... | collective-permute-start | bytes 55304 | tf_op jit(solution)/shard_map/while/body/eval_jaxpr/ppermute | solution.py:11
  129.3 1.9 collective-permute-start.1
  131.3 2.6 collective-permute-done.1
  134.0 9.8 %collective-permute-start = (f32[2,2,3,3,128]{4,1,3,2,0:T(2,128)S(1)}, f32[2,2,3,3,128]{4,1,3,2,0:T(2,128)S(1)}, u32[]{:S(2)}, u32[]{:S(2)}) collective-permute-start(f32[2,2,3,3,128]{4,1,3,2,0:T(2,128)S(1)} %get-tuple-element.507), channel_id=1, source_target_pairs={{16,0},{32,16},{48,32},{64,48},{80,64},{96,80},{112,96},{128,112},... | collective-permute-start | bytes 55304 | tf_op jit(solution)/shard_map/while/body/eval_jaxpr/ppermute | solution.py:11
  145.8 2.6 collective-permute-done.1
  148.5 9.8 %collective-permute-start = (f32[2,2,3,3,128]{4,1,3,2,0:T(2,128)S(1)}, f32[2,2,3,3,128]{4,1,3,2,0:T(2,128)S(1)}, u32[]{:S(2)}, u32[]{:S(2)}) collective-permute-start(f32[2,2,3,3,128]{4,1,3,2,0:T(2,128)S(1)} %get-tuple-element.507), channel_id=1, source_target_pairs={{16,0},{32,16},{48,32},{64,48},{80,64},{96,80},{112,96},{128,112},... | collective-permute-start | bytes 55304 | tf_op jit(solution)/shard_map/while/body/eval_jaxpr/ppermute | solution.py:11
  160.3 2.6 collective-permute-done.1
  163.1 9.8 %collective-permute-start = (f32[2,2,3,3,128]{4,1,3,2,0:T(2,128)S(1)}, f32[2,2,3,3,128]{4,1,3,2,0:T(2,128)S(1)}, u32[]{:S(2)}, u32[]{:S(2)}) collective-permute-start(f32[2,2,3,3,128]{4,1,3,2,0:T(2,128)S(1)} %get-tuple-element.507), channel_id=1, source_target_pairs={{16,0},{32,16},{48,32},{64,48},{80,64},{96,80},{112,96},{128,112},... | collective-permute-start | bytes 55304 | tf_op jit(solution)/shard_map/while/body/eval_jaxpr/ppermute | solution.py:11
  172.9 1.9 collective-permute-start.1
  174.9 2.6 collective-permute-done.1
  181.3 184.4 %while.51 = (s32[]{:T(128)}, f32[2,2,3,3,128]{4,0,3,2,1:T(2,128)}, f32[24,8,2,2,3,3,128]{6,1,5,4,3,2,0:T(8,128)S(1)}, f32[24,2,2,3,3,128]{5,1,4,3,2,0:T(2,128)},...) while((s32[]{:T(128)}, f32[2,2,3,3,128]{4,0,3,2,1:T(2,128)}, ...), condition=%wide.region_15.16_spmd, body=%wide.region_2.15_spmd.sunk | while | flops 910086 | bytes 2968279 | solution.py:63
  365.7 2.1 copy.70
  367.8 2.0 reshape.184
  369.8 3.3 fusion.5
  374.3 3.8 multiply_reduce_fusion.27
  379.4 4.2 fusion.7
  383.5 83.0 %psum.14 = f32[64,192]{1,0:T(8,128)S(1)} all-reduce(f32[64,192]{1,0:T(8,128)} %fusion.7), channel_id=1, replica_groups=mesh['gx'=32,'yz'=16] {'yz'}, use_global_device_ids=true, to_apply=%region_37.38 | all-reduce | flops 12288 | bytes 98304 | tf_op jit(solution)/shard_map/psum | solution.py:97
  466.6 167.1 %psum.15 = f32[64,192]{1,0:T(8,128)S(1)} all-reduce(f32[64,192]{1,0:T(8,128)S(1)} %psum.14), channel_id=1, replica_groups=mesh['gx'=32,'yz'=16] {'gx'}, use_global_device_ids=true, to_apply=%region_38.39 | all-reduce | flops 12288 | bytes 98304 | tf_op jit(solution)/shard_map/psum | solution.py:97
  635.0 4.7 fusion.6
  639.8 104.9 %while.52 = (s32[]{:T(128)}, f32[8,26,2,3,3,128]{5,0,4,3,2,1:T(8,128)S(1)}, s32[24]{0:T(128)S(1)}, f32[24,2,2,3,3,128]{5,1,4,3,2,0:T(2,128)}, f32[24,8,2,2,3,3,1...) while((s32[]{:T(128)}, f32[8,26,2,3,3,128]{5,0,4,3,2,1:T(8,128)S(1)}, s32[24]{0:T(128)S(1)}, ...), condition=%wide.region_34.35_spmd, body=%wide.region_25.34_spmd.sunk | while | flops 891653 | bytes 3411083 | solution.py:84
  746.0 2.9 rev.3
  749.0 159.1 %while.53 = (s32[]{:T(128)}, f32[8,2,2,3,3,128]{5,4,3,2,1,0:T(4,128)S(1)}, f32[12,8,2,2,3,3,128]{6,1,5,4,3,2,0:T(8,128)}, s32[]{:T(128)}) while((s32[]{:T(128)}, f32[8,2,2,3,3,128]{5,4,3,2,1,0:T(4,128)S(1)}, f32[12,8,2,2,3,3,128]{6,1,5,4,3,2,0:T(8,128)}, s32[]{:T(128)}) %tuple.163), condition=%wide.region_36.37_spmd, body=%wide.region_35.36_spmd.sunk | while | flops 36866 | bytes 1327209 | solution.py:93
  749.0 2.1 collective-permute-start.2
  752.0 11.9 %collective-permute-done.2 = f32[8,2,2,3,3,128]{5,4,3,2,1,0:T(4,128)S(1)} collective-permute-done((f32[8,2,2,3,3,128]{5,4,3,2,1,0:T(4,128)S(1)}, f32[8,2,2,3,3,128]{5,4,3,2,1,0:T(4,128)S(1)}, u32[]{:S(2)}, u32[]{:S(2)}) %collective-permute-start.2) | collective-permute-done | bytes 147488 | tf_op jit(solution)/shard_map/while/body/eval_jaxpr/ppermute | solution.py:11
  766.8 10.2 %collective-permute-done.2 = f32[8,2,2,3,3,128]{5,4,3,2,1,0:T(4,128)S(1)} collective-permute-done((f32[8,2,2,3,3,128]{5,4,3,2,1,0:T(4,128)S(1)}, f32[8,2,2,3,3,128]{5,4,3,2,1,0:T(4,128)S(1)}, u32[]{:S(2)}, u32[]{:S(2)}) %collective-permute-start.2) | collective-permute-done | bytes 147488 | tf_op jit(solution)/shard_map/while/body/eval_jaxpr/ppermute | solution.py:11
  777.1 1.9 collective-permute-start.2
  780.0 10.2 %collective-permute-done.2 = f32[8,2,2,3,3,128]{5,4,3,2,1,0:T(4,128)S(1)} collective-permute-done((f32[8,2,2,3,3,128]{5,4,3,2,1,0:T(4,128)S(1)}, f32[8,2,2,3,3,128]{5,4,3,2,1,0:T(4,128)S(1)}, u32[]{:S(2)}, u32[]{:S(2)}) %collective-permute-start.2) | collective-permute-done | bytes 147488 | tf_op jit(solution)/shard_map/while/body/eval_jaxpr/ppermute | solution.py:11
  793.1 10.1 %collective-permute-done.2 = f32[8,2,2,3,3,128]{5,4,3,2,1,0:T(4,128)S(1)} collective-permute-done((f32[8,2,2,3,3,128]{5,4,3,2,1,0:T(4,128)S(1)}, f32[8,2,2,3,3,128]{5,4,3,2,1,0:T(4,128)S(1)}, u32[]{:S(2)}, u32[]{:S(2)}) %collective-permute-start.2) | collective-permute-done | bytes 147488 | tf_op jit(solution)/shard_map/while/body/eval_jaxpr/ppermute | solution.py:11
  803.3 1.9 collective-permute-start.2
  806.2 10.1 %collective-permute-done.2 = f32[8,2,2,3,3,128]{5,4,3,2,1,0:T(4,128)S(1)} collective-permute-done((f32[8,2,2,3,3,128]{5,4,3,2,1,0:T(4,128)S(1)}, f32[8,2,2,3,3,128]{5,4,3,2,1,0:T(4,128)S(1)}, u32[]{:S(2)}, u32[]{:S(2)}) %collective-permute-start.2) | collective-permute-done | bytes 147488 | tf_op jit(solution)/shard_map/while/body/eval_jaxpr/ppermute | solution.py:11
  819.3 10.1 %collective-permute-done.2 = f32[8,2,2,3,3,128]{5,4,3,2,1,0:T(4,128)S(1)} collective-permute-done((f32[8,2,2,3,3,128]{5,4,3,2,1,0:T(4,128)S(1)}, f32[8,2,2,3,3,128]{5,4,3,2,1,0:T(4,128)S(1)}, u32[]{:S(2)}, u32[]{:S(2)}) %collective-permute-start.2) | collective-permute-done | bytes 147488 | tf_op jit(solution)/shard_map/while/body/eval_jaxpr/ppermute | solution.py:11
  832.4 10.1 %collective-permute-done.2 = f32[8,2,2,3,3,128]{5,4,3,2,1,0:T(4,128)S(1)} collective-permute-done((f32[8,2,2,3,3,128]{5,4,3,2,1,0:T(4,128)S(1)}, f32[8,2,2,3,3,128]{5,4,3,2,1,0:T(4,128)S(1)}, u32[]{:S(2)}, u32[]{:S(2)}) %collective-permute-start.2) | collective-permute-done | bytes 147488 | tf_op jit(solution)/shard_map/while/body/eval_jaxpr/ppermute | solution.py:11
  842.6 1.9 collective-permute-start.2
  845.5 10.1 %collective-permute-done.2 = f32[8,2,2,3,3,128]{5,4,3,2,1,0:T(4,128)S(1)} collective-permute-done((f32[8,2,2,3,3,128]{5,4,3,2,1,0:T(4,128)S(1)}, f32[8,2,2,3,3,128]{5,4,3,2,1,0:T(4,128)S(1)}, u32[]{:S(2)}, u32[]{:S(2)}) %collective-permute-start.2) | collective-permute-done | bytes 147488 | tf_op jit(solution)/shard_map/while/body/eval_jaxpr/ppermute | solution.py:11
  855.7 1.9 collective-permute-start.2
  858.5 10.1 %collective-permute-done.2 = f32[8,2,2,3,3,128]{5,4,3,2,1,0:T(4,128)S(1)} collective-permute-done((f32[8,2,2,3,3,128]{5,4,3,2,1,0:T(4,128)S(1)}, f32[8,2,2,3,3,128]{5,4,3,2,1,0:T(4,128)S(1)}, u32[]{:S(2)}, u32[]{:S(2)}) %collective-permute-start.2) | collective-permute-done | bytes 147488 | tf_op jit(solution)/shard_map/while/body/eval_jaxpr/ppermute | solution.py:11
  871.6 10.1 %collective-permute-done.2 = f32[8,2,2,3,3,128]{5,4,3,2,1,0:T(4,128)S(1)} collective-permute-done((f32[8,2,2,3,3,128]{5,4,3,2,1,0:T(4,128)S(1)}, f32[8,2,2,3,3,128]{5,4,3,2,1,0:T(4,128)S(1)}, u32[]{:S(2)}, u32[]{:S(2)}) %collective-permute-start.2) | collective-permute-done | bytes 147488 | tf_op jit(solution)/shard_map/while/body/eval_jaxpr/ppermute | solution.py:11
  884.7 10.1 %collective-permute-done.2 = f32[8,2,2,3,3,128]{5,4,3,2,1,0:T(4,128)S(1)} collective-permute-done((f32[8,2,2,3,3,128]{5,4,3,2,1,0:T(4,128)S(1)}, f32[8,2,2,3,3,128]{5,4,3,2,1,0:T(4,128)S(1)}, u32[]{:S(2)}, u32[]{:S(2)}) %collective-permute-start.2) | collective-permute-done | bytes 147488 | tf_op jit(solution)/shard_map/while/body/eval_jaxpr/ppermute | solution.py:11
  895.0 1.9 collective-permute-start.2
  897.8 10.1 %collective-permute-done.2 = f32[8,2,2,3,3,128]{5,4,3,2,1,0:T(4,128)S(1)} collective-permute-done((f32[8,2,2,3,3,128]{5,4,3,2,1,0:T(4,128)S(1)}, f32[8,2,2,3,3,128]{5,4,3,2,1,0:T(4,128)S(1)}, u32[]{:S(2)}, u32[]{:S(2)}) %collective-permute-start.2) | collective-permute-done | bytes 147488 | tf_op jit(solution)/shard_map/while/body/eval_jaxpr/ppermute | solution.py:11
  (1182 shorter events, 236.8 us)
Async XLA Ops:
  1.6 176.0 %copy-start.11 = (f32[2,2,3,3,128]{4,1,3,2,0:T(2,128)S(1)}, f32[2,2,3,3,128]{4,1,3,2,0:T(2,128)}, u32[]{:S(2)}) copy-start(f32[2,2,3,3,128]{4,1,3,2,0:T(2,128)} %param.12) | copy-start | bytes 55300
  2.4 12.5 %collective-permute-start = (f32[2,2,3,3,128]{4,1,3,2,0:T(2,128)S(1)}, f32[2,2,3,3,128]{4,1,3,2,0:T(2,128)S(1)}, u32[]{:S(2)}, u32[]{:S(2)}) collective-permute-start(f32[2,2,3,3,128]{4,1,3,2,0:T(2,128)S(1)} %get-tuple-element.507), channel_id=1, source_target_pairs={{16,0},{32,16},{48,32},{64,48},{80,64},{96,80},{112,96},{128,112},... | collective-permute-start | bytes 55304 | tf_op jit(solution)/shard_map/while/body/eval_jaxpr/ppermute | solution.py:11
  12.3 5.5 collective-permute-start.1
  17.9 11.7 %collective-permute-start = (f32[2,2,3,3,128]{4,1,3,2,0:T(2,128)S(1)}, f32[2,2,3,3,128]{4,1,3,2,0:T(2,128)S(1)}, u32[]{:S(2)}, u32[]{:S(2)}) collective-permute-start(f32[2,2,3,3,128]{4,1,3,2,0:T(2,128)S(1)} %get-tuple-element.507), channel_id=1, source_target_pairs={{16,0},{32,16},{48,32},{64,48},{80,64},{96,80},{112,96},{128,112},... | collective-permute-start | bytes 55304 | tf_op jit(solution)/shard_map/while/body/eval_jaxpr/ppermute | solution.py:11
  27.7 4.6 collective-permute-start.1
  32.4 11.8 %collective-permute-start = (f32[2,2,3,3,128]{4,1,3,2,0:T(2,128)S(1)}, f32[2,2,3,3,128]{4,1,3,2,0:T(2,128)S(1)}, u32[]{:S(2)}, u32[]{:S(2)}) collective-permute-start(f32[2,2,3,3,128]{4,1,3,2,0:T(2,128)S(1)} %get-tuple-element.507), channel_id=1, source_target_pairs={{16,0},{32,16},{48,32},{64,48},{80,64},{96,80},{112,96},{128,112},... | collective-permute-start | bytes 55304 | tf_op jit(solution)/shard_map/while/body/eval_jaxpr/ppermute | solution.py:11
  42.2 4.6 collective-permute-start.1
  46.9 11.8 %collective-permute-start = (f32[2,2,3,3,128]{4,1,3,2,0:T(2,128)S(1)}, f32[2,2,3,3,128]{4,1,3,2,0:T(2,128)S(1)}, u32[]{:S(2)}, u32[]{:S(2)}) collective-permute-start(f32[2,2,3,3,128]{4,1,3,2,0:T(2,128)S(1)} %get-tuple-element.507), channel_id=1, source_target_pairs={{16,0},{32,16},{48,32},{64,48},{80,64},{96,80},{112,96},{128,112},... | collective-permute-start | bytes 55304 | tf_op jit(solution)/shard_map/while/body/eval_jaxpr/ppermute | solution.py:11
  56.7 4.6 collective-permute-start.1
  61.4 11.8 %collective-permute-start = (f32[2,2,3,3,128]{4,1,3,2,0:T(2,128)S(1)}, f32[2,2,3,3,128]{4,1,3,2,0:T(2,128)S(1)}, u32[]{:S(2)}, u32[]{:S(2)}) collective-permute-start(f32[2,2,3,3,128]{4,1,3,2,0:T(2,128)S(1)} %get-tuple-element.507), channel_id=1, source_target_pairs={{16,0},{32,16},{48,32},{64,48},{80,64},{96,80},{112,96},{128,112},... | collective-permute-start | bytes 55304 | tf_op jit(solution)/shard_map/while/body/eval_jaxpr/ppermute | solution.py:11
  71.2 4.6 collective-permute-start.1
  75.9 11.8 %collective-permute-start = (f32[2,2,3,3,128]{4,1,3,2,0:T(2,128)S(1)}, f32[2,2,3,3,128]{4,1,3,2,0:T(2,128)S(1)}, u32[]{:S(2)}, u32[]{:S(2)}) collective-permute-start(f32[2,2,3,3,128]{4,1,3,2,0:T(2,128)S(1)} %get-tuple-element.507), channel_id=1, source_target_pairs={{16,0},{32,16},{48,32},{64,48},{80,64},{96,80},{112,96},{128,112},... | collective-permute-start | bytes 55304 | tf_op jit(solution)/shard_map/while/body/eval_jaxpr/ppermute | solution.py:11
  85.8 4.6 collective-permute-start.1
  90.5 11.8 %collective-permute-start = (f32[2,2,3,3,128]{4,1,3,2,0:T(2,128)S(1)}, f32[2,2,3,3,128]{4,1,3,2,0:T(2,128)S(1)}, u32[]{:S(2)}, u32[]{:S(2)}) collective-permute-start(f32[2,2,3,3,128]{4,1,3,2,0:T(2,128)S(1)} %get-tuple-element.507), channel_id=1, source_target_pairs={{16,0},{32,16},{48,32},{64,48},{80,64},{96,80},{112,96},{128,112},... | collective-permute-start | bytes 55304 | tf_op jit(solution)/shard_map/while/body/eval_jaxpr/ppermute | solution.py:11
  100.3 4.6 collective-permute-start.1
  105.0 11.8 %collective-permute-start = (f32[2,2,3,3,128]{4,1,3,2,0:T(2,128)S(1)}, f32[2,2,3,3,128]{4,1,3,2,0:T(2,128)S(1)}, u32[]{:S(2)}, u32[]{:S(2)}) collective-permute-start(f32[2,2,3,3,128]{4,1,3,2,0:T(2,128)S(1)} %get-tuple-element.507), channel_id=1, source_target_pairs={{16,0},{32,16},{48,32},{64,48},{80,64},{96,80},{112,96},{128,112},... | collective-permute-start | bytes 55304 | tf_op jit(solution)/shard_map/while/body/eval_jaxpr/ppermute | solution.py:11
  114.8 4.6 collective-permute-start.1
  119.5 11.8 %collective-permute-start = (f32[2,2,3,3,128]{4,1,3,2,0:T(2,128)S(1)}, f32[2,2,3,3,128]{4,1,3,2,0:T(2,128)S(1)}, u32[]{:S(2)}, u32[]{:S(2)}) collective-permute-start(f32[2,2,3,3,128]{4,1,3,2,0:T(2,128)S(1)} %get-tuple-element.507), channel_id=1, source_target_pairs={{16,0},{32,16},{48,32},{64,48},{80,64},{96,80},{112,96},{128,112},... | collective-permute-start | bytes 55304 | tf_op jit(solution)/shard_map/while/body/eval_jaxpr/ppermute | solution.py:11
  129.3 4.6 collective-permute-start.1
  134.0 11.8 %collective-permute-start = (f32[2,2,3,3,128]{4,1,3,2,0:T(2,128)S(1)}, f32[2,2,3,3,128]{4,1,3,2,0:T(2,128)S(1)}, u32[]{:S(2)}, u32[]{:S(2)}) collective-permute-start(f32[2,2,3,3,128]{4,1,3,2,0:T(2,128)S(1)} %get-tuple-element.507), channel_id=1, source_target_pairs={{16,0},{32,16},{48,32},{64,48},{80,64},{96,80},{112,96},{128,112},... | collective-permute-start | bytes 55304 | tf_op jit(solution)/shard_map/while/body/eval_jaxpr/ppermute | solution.py:11
  143.8 4.6 collective-permute-start.1
  148.5 11.8 %collective-permute-start = (f32[2,2,3,3,128]{4,1,3,2,0:T(2,128)S(1)}, f32[2,2,3,3,128]{4,1,3,2,0:T(2,128)S(1)}, u32[]{:S(2)}, u32[]{:S(2)}) collective-permute-start(f32[2,2,3,3,128]{4,1,3,2,0:T(2,128)S(1)} %get-tuple-element.507), channel_id=1, source_target_pairs={{16,0},{32,16},{48,32},{64,48},{80,64},{96,80},{112,96},{128,112},... | collective-permute-start | bytes 55304 | tf_op jit(solution)/shard_map/while/body/eval_jaxpr/ppermute | solution.py:11
  158.4 4.6 collective-permute-start.1
  163.1 11.8 %collective-permute-start = (f32[2,2,3,3,128]{4,1,3,2,0:T(2,128)S(1)}, f32[2,2,3,3,128]{4,1,3,2,0:T(2,128)S(1)}, u32[]{:S(2)}, u32[]{:S(2)}) collective-permute-start(f32[2,2,3,3,128]{4,1,3,2,0:T(2,128)S(1)} %get-tuple-element.507), channel_id=1, source_target_pairs={{16,0},{32,16},{48,32},{64,48},{80,64},{96,80},{112,96},{128,112},... | collective-permute-start | bytes 55304 | tf_op jit(solution)/shard_map/while/body/eval_jaxpr/ppermute | solution.py:11
  172.9 4.6 collective-permute-start.1
  184.0 2.7 copy-start.3
  191.7 2.7 copy-start.3
  199.4 2.7 copy-start.3
  207.0 2.7 copy-start.3
  214.7 2.7 copy-start.3
  222.4 2.7 copy-start.3
  230.1 2.7 copy-start.3
  237.8 2.7 copy-start.3
  245.5 2.7 copy-start.3
  253.2 2.7 copy-start.3
  260.9 2.7 copy-start.3
  268.6 2.7 copy-start.3
  276.3 2.7 copy-start.3
  283.9 2.7 copy-start.3
  291.6 2.7 copy-start.3
  299.3 2.7 copy-start.3
  307.0 2.7 copy-start.3
  314.7 2.7 copy-start.3
  322.4 2.7 copy-start.3
  330.1 2.7 copy-start.3
  337.8 2.7 copy-start.3
  345.4 2.7 copy-start.3
  383.5 251.4 %copy-start.1 = (f32[8,8,2,2,3,3,128]{6,1,5,4,3,2,0:T(8,128)S(1)}, f32[8,8,2,2,3,3,128]{6,1,5,4,3,2,0:T(8,128)}, u32[]{:S(2)}) copy-start(f32[8,8,2,2,3,3,128]{6,1,5,4,3,2,0:T(8,128)} %copy-done) | copy-start | bytes 3538948
  383.5 251.4 %copy-start.9 = (f32[64,192]{1,0:T(8,128)S(1)}, f32[64,192]{1,0:T(8,128)}, u32[]{:S(2)}) copy-start(f32[64,192]{1,0:T(8,128)} %reshape.184) | copy-start | bytes 147460
  746.0 162.0 %copy-start.6 = (f32[8,8,2,3,3,128]{5,1,4,3,2,0:T(8,128)S(1)}, f32[8,8,2,3,3,128]{5,1,4,3,2,0:T(8,128)}, u32[]{:S(2)}) copy-start(f32[8,8,2,3,3,128]{5,1,4,3,2,0:T(8,128)} %get-tuple-element.198) | copy-start | bytes 1769476
  748.9 159.2 %copy-start.5 = (f32[8,8,2,3,3,128]{5,1,4,3,2,0:T(8,128)S(1)}, f32[8,8,2,3,3,128]{5,1,4,3,2,0:T(8,128)}, u32[]{:S(2)}) copy-start(f32[8,8,2,3,3,128]{5,1,4,3,2,0:T(8,128)} %get-tuple-element.197) | copy-start | bytes 1769476
  749.0 159.1 %copy-start.4 = (f32[8,8,2,3,3,128]{5,1,4,3,2,0:T(8,128)S(1)}, f32[8,8,2,3,3,128]{5,1,4,3,2,0:T(8,128)}, u32[]{:S(2)}) copy-start(f32[8,8,2,3,3,128]{5,1,4,3,2,0:T(8,128)} %get-tuple-element.196) | copy-start | bytes 1769476
  749.0 14.9 %collective-permute-start.2 = (f32[8,2,2,3,3,128]{5,4,3,2,1,0:T(4,128)S(1)}, f32[8,2,2,3,3,128]{5,4,3,2,1,0:T(4,128)S(1)}, u32[]{:S(2)}, u32[]{:S(2)}) collective-permute-start(f32[8,2,2,3,3,128]{5,4,3,2,1,0:T(4,128)S(1)} %get-tuple-element.580), channel_id=1, source_target_pairs={{496,0},{0,16},{16,32},{32,48},{48,64},{64,80},{80,96},{96,112},{1... | collective-permute-start | bytes 442376 | tf_op jit(solution)/shard_map/while/body/eval_jaxpr/ppermute | solution.py:11
  763.9 13.1 %collective-permute-start.2 = (f32[8,2,2,3,3,128]{5,4,3,2,1,0:T(4,128)S(1)}, f32[8,2,2,3,3,128]{5,4,3,2,1,0:T(4,128)S(1)}, u32[]{:S(2)}, u32[]{:S(2)}) collective-permute-start(f32[8,2,2,3,3,128]{5,4,3,2,1,0:T(4,128)S(1)} %get-tuple-element.580), channel_id=1, source_target_pairs={{496,0},{0,16},{16,32},{32,48},{48,64},{64,80},{80,96},{96,112},{1... | collective-permute-start | bytes 442376 | tf_op jit(solution)/shard_map/while/body/eval_jaxpr/ppermute | solution.py:11
  777.1 13.0 %collective-permute-start.2 = (f32[8,2,2,3,3,128]{5,4,3,2,1,0:T(4,128)S(1)}, f32[8,2,2,3,3,128]{5,4,3,2,1,0:T(4,128)S(1)}, u32[]{:S(2)}, u32[]{:S(2)}) collective-permute-start(f32[8,2,2,3,3,128]{5,4,3,2,1,0:T(4,128)S(1)} %get-tuple-element.580), channel_id=1, source_target_pairs={{496,0},{0,16},{16,32},{32,48},{48,64},{64,80},{80,96},{96,112},{1... | collective-permute-start | bytes 442376 | tf_op jit(solution)/shard_map/while/body/eval_jaxpr/ppermute | solution.py:11
  790.2 13.0 %collective-permute-start.2 = (f32[8,2,2,3,3,128]{5,4,3,2,1,0:T(4,128)S(1)}, f32[8,2,2,3,3,128]{5,4,3,2,1,0:T(4,128)S(1)}, u32[]{:S(2)}, u32[]{:S(2)}) collective-permute-start(f32[8,2,2,3,3,128]{5,4,3,2,1,0:T(4,128)S(1)} %get-tuple-element.580), channel_id=1, source_target_pairs={{496,0},{0,16},{16,32},{32,48},{48,64},{64,80},{80,96},{96,112},{1... | collective-permute-start | bytes 442376 | tf_op jit(solution)/shard_map/while/body/eval_jaxpr/ppermute | solution.py:11
  803.3 13.0 %collective-permute-start.2 = (f32[8,2,2,3,3,128]{5,4,3,2,1,0:T(4,128)S(1)}, f32[8,2,2,3,3,128]{5,4,3,2,1,0:T(4,128)S(1)}, u32[]{:S(2)}, u32[]{:S(2)}) collective-permute-start(f32[8,2,2,3,3,128]{5,4,3,2,1,0:T(4,128)S(1)} %get-tuple-element.580), channel_id=1, source_target_pairs={{496,0},{0,16},{16,32},{32,48},{48,64},{64,80},{80,96},{96,112},{1... | collective-permute-start | bytes 442376 | tf_op jit(solution)/shard_map/while/body/eval_jaxpr/ppermute | solution.py:11
  816.4 13.0 %collective-permute-start.2 = (f32[8,2,2,3,3,128]{5,4,3,2,1,0:T(4,128)S(1)}, f32[8,2,2,3,3,128]{5,4,3,2,1,0:T(4,128)S(1)}, u32[]{:S(2)}, u32[]{:S(2)}) collective-permute-start(f32[8,2,2,3,3,128]{5,4,3,2,1,0:T(4,128)S(1)} %get-tuple-element.580), channel_id=1, source_target_pairs={{496,0},{0,16},{16,32},{32,48},{48,64},{64,80},{80,96},{96,112},{1... | collective-permute-start | bytes 442376 | tf_op jit(solution)/shard_map/while/body/eval_jaxpr/ppermute | solution.py:11
  829.5 13.0 %collective-permute-start.2 = (f32[8,2,2,3,3,128]{5,4,3,2,1,0:T(4,128)S(1)}, f32[8,2,2,3,3,128]{5,4,3,2,1,0:T(4,128)S(1)}, u32[]{:S(2)}, u32[]{:S(2)}) collective-permute-start(f32[8,2,2,3,3,128]{5,4,3,2,1,0:T(4,128)S(1)} %get-tuple-element.580), channel_id=1, source_target_pairs={{496,0},{0,16},{16,32},{32,48},{48,64},{64,80},{80,96},{96,112},{1... | collective-permute-start | bytes 442376 | tf_op jit(solution)/shard_map/while/body/eval_jaxpr/ppermute | solution.py:11
  842.6 13.0 %collective-permute-start.2 = (f32[8,2,2,3,3,128]{5,4,3,2,1,0:T(4,128)S(1)}, f32[8,2,2,3,3,128]{5,4,3,2,1,0:T(4,128)S(1)}, u32[]{:S(2)}, u32[]{:S(2)}) collective-permute-start(f32[8,2,2,3,3,128]{5,4,3,2,1,0:T(4,128)S(1)} %get-tuple-element.580), channel_id=1, source_target_pairs={{496,0},{0,16},{16,32},{32,48},{48,64},{64,80},{80,96},{96,112},{1... | collective-permute-start | bytes 442376 | tf_op jit(solution)/shard_map/while/body/eval_jaxpr/ppermute | solution.py:11
  855.7 13.0 %collective-permute-start.2 = (f32[8,2,2,3,3,128]{5,4,3,2,1,0:T(4,128)S(1)}, f32[8,2,2,3,3,128]{5,4,3,2,1,0:T(4,128)S(1)}, u32[]{:S(2)}, u32[]{:S(2)}) collective-permute-start(f32[8,2,2,3,3,128]{5,4,3,2,1,0:T(4,128)S(1)} %get-tuple-element.580), channel_id=1, source_target_pairs={{496,0},{0,16},{16,32},{32,48},{48,64},{64,80},{80,96},{96,112},{1... | collective-permute-start | bytes 442376 | tf_op jit(solution)/shard_map/while/body/eval_jaxpr/ppermute | solution.py:11
  868.8 13.0 %collective-permute-start.2 = (f32[8,2,2,3,3,128]{5,4,3,2,1,0:T(4,128)S(1)}, f32[8,2,2,3,3,128]{5,4,3,2,1,0:T(4,128)S(1)}, u32[]{:S(2)}, u32[]{:S(2)}) collective-permute-start(f32[8,2,2,3,3,128]{5,4,3,2,1,0:T(4,128)S(1)} %get-tuple-element.580), channel_id=1, source_target_pairs={{496,0},{0,16},{16,32},{32,48},{48,64},{64,80},{80,96},{96,112},{1... | collective-permute-start | bytes 442376 | tf_op jit(solution)/shard_map/while/body/eval_jaxpr/ppermute | solution.py:11
  881.9 13.0 %collective-permute-start.2 = (f32[8,2,2,3,3,128]{5,4,3,2,1,0:T(4,128)S(1)}, f32[8,2,2,3,3,128]{5,4,3,2,1,0:T(4,128)S(1)}, u32[]{:S(2)}, u32[]{:S(2)}) collective-permute-start(f32[8,2,2,3,3,128]{5,4,3,2,1,0:T(4,128)S(1)} %get-tuple-element.580), channel_id=1, source_target_pairs={{496,0},{0,16},{16,32},{32,48},{48,64},{64,80},{80,96},{96,112},{1... | collective-permute-start | bytes 442376 | tf_op jit(solution)/shard_map/while/body/eval_jaxpr/ppermute | solution.py:11
  895.0 13.0 %collective-permute-start.2 = (f32[8,2,2,3,3,128]{5,4,3,2,1,0:T(4,128)S(1)}, f32[8,2,2,3,3,128]{5,4,3,2,1,0:T(4,128)S(1)}, u32[]{:S(2)}, u32[]{:S(2)}) collective-permute-start(f32[8,2,2,3,3,128]{5,4,3,2,1,0:T(4,128)S(1)} %get-tuple-element.580), channel_id=1, source_target_pairs={{496,0},{0,16},{16,32},{32,48},{48,64},{64,80},{80,96},{96,112},{1... | collective-permute-start | bytes 442376 | tf_op jit(solution)/shard_map/while/body/eval_jaxpr/ppermute | solution.py:11
  (7 other events, 9.9 us)
